TPU v7x, 256 devices: a whole 4x4x8 slice. The times are simulated.
256 devices in a mesh: dp: 8 (over z_hi, core), expert: 32 (over x, z_lo, y).
Axes of the slice: x: 4, y: 4, z: 8 (z_hi: 4, z_lo: 2; z = z_hi * 2 + z_lo), core: 2. Of those that a mesh axis runs over, the one named last changes fastest.
Arguments:
- tokens: bfloat16 [256, 256, 1024], P(('dp', 'expert'))
- router: bfloat16 [1024, 128], replicated
- weight_in: bfloat16 [128, 1024, 2048], P('expert', None, 'dp'), may hold values from -0.1875 to 0.1875
- weight_out: bfloat16 [128, 2048, 1024], P('expert', 'dp'), may hold values from -0.125 to 0.125
- cotangent: bfloat16 [256, 256, 1024], P(('dp', 'expert')), may hold values from -6 to 6
Outputs:
- mixed: bfloat16 [256, 256, 1024], P(('dp', 'expert'))
- grad_tokens: bfloat16 [256, 256, 1024], P(('dp', 'expert'))
- grad_router: float32 [1024, 128], replicated
- grad_weight_in: bfloat16 [128, 1024, 2048], P('expert', None, 'dp')
- grad_weight_out: bfloat16 [128, 2048, 1024], P('expert', 'dp')
All inputs are finite; a program needn't handle non-finite values.
Results may differ from a plain program's by a relative error of at most 0.018.
Values may be sent and summed in bfloat16 or wider, within the bound.
A program may use at most 64 MiB of HBM per device.

v0:
```python
import jax
import jax.numpy as jnp
from jax import lax
from jax.sharding import PartitionSpec as P


def gelu_exact(values):
    return jax.nn.gelu(values, approximate=False)


def local(tokens, router, weight_in, weight_out, cotangent):
    experts_dev = weight_in.shape[0]
    width = tokens.shape[2]
    logits = jnp.einsum("isd,de->ise", tokens, router, preferred_element_type=jnp.float32)
    dispatch_prob = jax.nn.softmax(logits, axis=1)
    combine_prob = jax.nn.softmax(logits, axis=2)
    dispatch = dispatch_prob.astype(jnp.bfloat16)
    combine = combine_prob.astype(jnp.bfloat16)
    slots = jnp.einsum("ise,isd->ied", dispatch, tokens, preferred_element_type=jnp.float32).astype(
        jnp.bfloat16
    )
    grad_slots = jnp.einsum(
        "ise,isd->ied", combine, cotangent, preferred_element_type=jnp.float32
    ).astype(jnp.bfloat16)

    def to_owners(local_rows):
        arrived = lax.all_to_all(local_rows, "expert", split_axis=1, concat_axis=1, tiled=True)
        return lax.all_gather(arrived, "dp", axis=0, tiled=True)

    def from_owners(partial_value):
        summed = lax.psum_scatter(partial_value, "dp", scatter_dimension=0, tiled=True).astype(
            jnp.float32
        )
        return lax.all_to_all(
            summed.astype(jnp.bfloat16), "expert", split_axis=1, concat_axis=1, tiled=True
        )

    slot_rows = to_owners(slots)
    blocks = slot_rows.reshape(-1, experts_dev, width)
    pre_act = jnp.einsum("rkd,kdf->rkf", blocks, weight_in, preferred_element_type=jnp.float32)
    hidden = gelu_exact(pre_act).astype(jnp.bfloat16)
    partial_value = jnp.einsum(
        "rkf,kfd->rkd", hidden, weight_out, preferred_element_type=jnp.float32
    )
    blocks, pre_act, hidden, partial_value = (
        blocks,
        pre_act,
        hidden,
        partial_value.astype(jnp.bfloat16).reshape(slot_rows.shape),
    )
    expert_outs = from_owners(partial_value)
    grad_rows = to_owners(grad_slots)
    grad_blocks = grad_rows.reshape(blocks.shape)
    grad_hidden = jnp.einsum(
        "rkd,kfd->rkf", grad_blocks, weight_out, preferred_element_type=jnp.float32
    )
    _, gelu_back = jax.vjp(gelu_exact, pre_act)
    grad_pre = gelu_back(grad_hidden)[0].astype(jnp.bfloat16)
    grad_second = jnp.einsum(
        "rkf,rkd->kfd", hidden, grad_blocks, preferred_element_type=jnp.float32
    ).astype(jnp.bfloat16)
    grad_first = jnp.einsum(
        "rkd,rkf->kdf", blocks, grad_pre, preferred_element_type=jnp.float32
    ).astype(jnp.bfloat16)
    partial_back = jnp.einsum(
        "rkf,kdf->rkd", grad_pre, weight_in, preferred_element_type=jnp.float32
    )
    grad_first, grad_second, partial_back = (
        grad_first,
        grad_second,
        partial_back.astype(jnp.bfloat16).reshape(grad_rows.shape),
    )
    grad_slot_all = from_owners(partial_back)
    mixed = jnp.einsum(
        "ise,ied->isd", combine, expert_outs, preferred_element_type=jnp.float32
    ).astype(jnp.bfloat16)
    grad_comb = jnp.einsum(
        "isd,ied->ise", cotangent, expert_outs, preferred_element_type=jnp.float32
    )
    grad_disp = jnp.einsum(
        "isd,ied->ise", tokens, grad_slot_all, preferred_element_type=jnp.float32
    )
    part_disp = dispatch_prob * (
        grad_disp - jnp.sum(dispatch_prob * grad_disp, axis=1, keepdims=True)
    )
    part_comb = combine_prob * (
        grad_comb - jnp.sum(combine_prob * grad_comb, axis=2, keepdims=True)
    )
    grad_logits = (part_disp + part_comb).astype(jnp.bfloat16)
    grad_tokens = (
        jnp.einsum("ise,ied->isd", dispatch, grad_slot_all, preferred_element_type=jnp.float32)
        + jnp.einsum("ise,de->isd", grad_logits, router, preferred_element_type=jnp.float32)
    ).astype(jnp.bfloat16)
    router_term = jnp.einsum("isd,ise->de", tokens, grad_logits, preferred_element_type=jnp.float32)
    grad_router = lax.psum(router_term, ("dp", "expert"))
    return (mixed, grad_tokens, grad_router, grad_first, grad_second)


def solution(mesh):
    return jax.shard_map(
        local,
        mesh=mesh,
        in_specs=(
            P(("dp", "expert"), None, None),
            P(),
            P("expert", None, "dp"),
            P("expert", "dp", None),
            P(("dp", "expert"), None, None),
        ),
        out_specs=(
            P(("dp", "expert"), None, None),
            P(("dp", "expert"), None, None),
            P(),
            P("expert", None, "dp"),
            P("expert", "dp", None),
        ),
        check_vma=False,
    )
```

profile of v0, /device:TPU:2, one launch (start us, length us, event | category | flops | bytes accessed | tf_op | source)
XLA Modules:
  0.0 497.0 jit_solution(17294189357701382762)
XLA Ops:
  13.6 16.7 %all_to_all.20 = bf16[32,2,2048]{2,1,0:T(2,128)(2,1)S(1)} all-to-all(bf16[32,2,2048]{2,1,0:T(2,128)(2,1)S(1)} %reshape.119), channel_id=1, replica_groups=mesh['dp'=8,'expert'=32] {'expert'}, dimensions={0} | all-to-all | bytes 524288 | tf_op jit(solution)/shard_map/all_to_all | solution.py:27
  34.6 12.8 %all_to_all.21 = bf16[32,2,2048]{2,1,0:T(2,128)(2,1)S(1)} all-to-all(bf16[32,2,2048]{2,1,0:T(2,128)(2,1)S(1)} %reshape.123), channel_id=1, replica_groups=mesh['dp'=8,'expert'=32] {'expert'}, dimensions={0} | all-to-all | bytes 524288 | tf_op jit(solution)/shard_map/all_to_all | solution.py:27
  48.7 18.3 %all-gather.3.cloned.1.call-done = bf16[8,128,1024]{2,1,0:T(8,128)(2,1)} async-done(((bf16[1,128,1024]{2,1,0:T(8,128)(2,1)}), bf16[8,128,1024]{2,1,0:T(8,128)(2,1)}) %all-gather.3.cloned.1.call-update) | async-done | bytes 2097168 | tf_op jit(solution)/shard_map/all_gather | solution.py:28
  67.0 4.1 reshape.112
  71.1 4.3 copy.53
  75.4 5.3 %fusion.13 = (bf16[256,4,256]{2,0,1:T(8,128)(2,1)S(1)}, f32[4,256,256]{2,1,0:T(8,128)}) fusion(bf16[256,4,1024]{0,2,1:T(8,128)(2,1)} %copy.53, bf16[4,1024,256]{2,1,0:T(8,128)(2,1)S(1)} %copy-done), kind=kOutput, calls=%fused_computation.29 | convolution fusion | flops 553910272 | bytes 5767168 | tf_op jit(solution)/shard_map/rkd,kdf->rkf/dot_general | solution.py:40
  80.7 23.0 %all-gather.5.cloned.1.call-done = bf16[8,128,1024]{2,1,0:T(8,128)(2,1)} async-done(((bf16[1,128,1024]{2,1,0:T(8,128)(2,1)}), bf16[8,128,1024]{2,1,0:T(8,128)(2,1)}) %all-gather.5.cloned.1.call-update) | async-done | bytes 2097168 | tf_op jit(solution)/shard_map/all_gather | solution.py:28
  103.7 4.1 reshape.116
  107.8 5.7 %fusion.19 = bf16[256,4,256]{2,0,1:T(8,128)(2,1)S(1)} fusion(bf16[4,256,1024]{2,1,0:T(8,128)(2,1)} %param.8, bf16[256,4,1024]{2,1,0:T(4,128)(2,1)} %reshape.116, f32[4,256,256]{2,1,0:T(8,128)} %get-tuple-element.33), kind=kOutput, calls=%fused_computation.35 | convolution fusion | flops 555745280 | bytes 5767168 | tf_op jit(solution)/shard_map/rkd,kfd->rkf/dot_general | solution.py:54
  114.3 2.9 copy.49
  117.2 4.0 reshape.117
  121.5 2.3 convert_bitcast_fusion.1
  123.8 2.9 copy.44
  126.8 3.9 reshape.113
  130.7 31.9 %reduce-scatter.5.cloned.1.call-done = bf16[1,128,1024]{2,1,0:T(8,128)(2,1)} async-done(((bf16[8,128,1024]{2,1,0:T(8,128)(2,1)}), bf16[1,128,1024]{2,1,0:T(8,128)(2,1)}) %reduce-scatter.5.cloned.1.call-update) | async-done | bytes 262160 | tf_op jit(solution)/shard_map/reduce_scatter | solution.py:31
  164.8 3.1 reduce.15
  168.8 7.7 %all-to-all-start.3 = ((bf16[32,2,2048]{2,1,0:T(2,128)(2,1)}), bf16[32,2,2048]{2,1,0:T(2,128)(2,1)S(1)}, u32[]{:S(2)}, u32[]{:S(2)}) async-start(bf16[32,2,2048]{2,1,0:T(2,128)(2,1)} %reshape.125), calls=%async_computation.5 | async-start | bytes 524288 | tf_op jit(solution)/shard_map/all_to_all | solution.py:34
  176.5 4.5 convolution_convert_fusion
  181.0 28.3 %reduce-scatter.3.cloned.1.call-done = bf16[1,128,1024]{2,1,0:T(8,128)(2,1)} async-done(((bf16[8,128,1024]{2,1,0:T(8,128)(2,1)}), bf16[1,128,1024]{2,1,0:T(8,128)(2,1)}) %reduce-scatter.3.cloned.1.call-update) | async-done | bytes 262160 | tf_op jit(solution)/shard_map/reduce_scatter | solution.py:31
  210.7 2.9 reduce.13
  215.4 7.4 %all-to-all-start.1 = ((bf16[32,2,2048]{2,1,0:T(2,128)(2,1)}), bf16[32,2,2048]{2,1,0:T(2,128)(2,1)}, u32[]{:S(2)}, u32[]{:S(2)}) async-start(bf16[32,2,2048]{2,1,0:T(2,128)(2,1)} %reshape.121), calls=%async_computation.2 | async-start | bytes 524288 | tf_op jit(solution)/shard_map/all_to_all | solution.py:34
  223.1 3.6 convolution_convert_fusion.1
  230.8 2.8 reshape.122
  243.1 245.3 %all-reduce.2.cloned.1.call-done = f32[1024,128]{0,1:T(8,128)} async-done(((f32[1024,128]{0,1:T(8,128)}), f32[1024,128]{0,1:T(8,128)}) %all-reduce.2.cloned.1.call-update) | async-done | bytes 524304 | tf_op jit(solution)/shard_map/psum | solution.py:95
  (56 shorter events, 34.9 us)
Async XLA Ops:
  7.2 68.3 %copy-start = (bf16[4,1024,256]{2,1,0:T(8,128)(2,1)S(1)}, bf16[4,1024,256]{2,1,0:T(8,128)(2,1)}, u32[]{:S(2)}) copy-start(bf16[4,1024,256]{2,1,0:T(8,128)(2,1)} %param.7) | copy-start | bytes 6291460
  7.2 59.8 %all-gather.3.cloned.1.call-start = ((), (), s32[]{:S(2)}) async-start(), calls=%async_computation.6 | async-start | bytes 2359296 | tf_op jit(solution)/shard_map/all_gather | solution.py:28
  10.4 21.1 %copy-start.1 = (bf16[1,256,1024]{2,1,0:T(8,128)(2,1)S(1)}, bf16[1,256,1024]{2,1,0:T(8,128)(2,1)}, u32[]{:S(2)}) copy-start(bf16[1,256,1024]{2,1,0:T(8,128)(2,1)} %param.9) | copy-start | bytes 1572868
  31.4 72.2 %all-gather.5.cloned.1.call-start = ((), (), s32[]{:S(2)}) async-start(), calls=%async_computation.8 | async-start | bytes 2359296 | tf_op jit(solution)/shard_map/all_gather | solution.py:28
  48.5 114.1 %reduce-scatter.5.cloned.1.call-start = ((), (), s32[]{:S(2)}) async-start(), calls=%async_computation.9 | async-start | bytes 2359296 | tf_op jit(solution)/shard_map/reduce_scatter | solution.py:31
  121.2 88.1 %reduce-scatter.3.cloned.1.call-start = ((), (), s32[]{:S(2)}) async-start(), calls=%async_computation.7 | async-start | bytes 2359296 | tf_op jit(solution)/shard_map/reduce_scatter | solution.py:31
  168.8 46.6 %all-to-all-start.3 = ((bf16[32,2,2048]{2,1,0:T(2,128)(2,1)}), bf16[32,2,2048]{2,1,0:T(2,128)(2,1)S(1)}, u32[]{:S(2)}, u32[]{:S(2)}) async-start(bf16[32,2,2048]{2,1,0:T(2,128)(2,1)} %reshape.125), calls=%async_computation.5 | async-start | bytes 524288 | tf_op jit(solution)/shard_map/all_to_all | solution.py:34
  215.4 15.4 %all-to-all-start.1 = ((bf16[32,2,2048]{2,1,0:T(2,128)(2,1)}), bf16[32,2,2048]{2,1,0:T(2,128)(2,1)}, u32[]{:S(2)}, u32[]{:S(2)}) async-start(bf16[32,2,2048]{2,1,0:T(2,128)(2,1)} %reshape.121), calls=%async_computation.2 | async-start | bytes 524288 | tf_op jit(solution)/shard_map/all_to_all | solution.py:34
  222.8 265.6 %all-reduce.2.cloned.1.call-start = ((), (), s32[]{:S(2)}) async-start(), calls=%async_computation.10 | async-start | bytes 1048576 | tf_op jit(solution)/shard_map/psum | solution.py:95
  233.6 3.9 copy-start.2
  235.2 1.6 copy-start.4
  235.2 5.7 %copy-start.3 = (bf16[1024,128]{1,0:T(8,128)(2,1)S(1)}, bf16[1024,128]{1,0:T(8,128)(2,1)}, u32[]{:S(2)}) copy-start(bf16[1024,128]{1,0:T(8,128)(2,1)} %param.6) | copy-start | bytes 786436
  236.8 0.7 copy-start.5
  236.8 0.7 copy-start.6
  236.8 0.6 copy-start.7
Sparse Core Ops, SparseCore 0:
  31.6 35.4 all-gather.2
  69.5 34.1 all-gather.4
  121.4 41.2 reduce-scatter.4
  165.6 43.6 reduce-scatter.2
  238.8 249.5 all-reduce.1
where the time goes:
time: 498 us; the launch traced here: 497 us
  waiting for transfers between devices  349 us (70%)
  local copies, waits for them, and re-layouts  42.7 us (9%)
  matrix products  35.6 us (7%)
  blocking collectives  29.5 us (6%)
  starting transfers between devices  16 us (3%)
  between operations  14 us (3%)
  other arithmetic  10.5 us (2%)
    psum x1, waiting for transfers between devices, local(): grad_router = lax.psum(router_term, ('dp', 'expert'))  245 us
    reduce_scatter x2, waiting for transfers between devices, from_owners(): lax.psum_scatter(partial_value, 'dp', scatter_dimension=0, tiled=True)  60.2 us
    all_gather x2, waiting for transfers between devices, to_owners(): return lax.all_gather(arrived, 'dp', axis=0, tiled=True)  41.3 us
    all_to_all x2, blocking collectives, to_owners(): lax.all_to_all(local_rows, 'expert', split_axis=1, concat_axis=1, tiled=T...  29.5 us
    all_to_all x2, starting transfers between devices, from_owners(): lax.all_to_all(summed.astype(jnp.bfloat16), 'expert', split_axis=1, conca...  15.1 us
    unnamed x26, local copies, waits for them, and re-layouts  10.5 us
    unnamed x4, other arithmetic  10.3 us
  transfers between devices with their start and end apart: 7, of which 6 were waited for; matrix products, arithmetic and copies ran while one was open for 11% of the time, Pallas kernels for 0%

commit v1 on v0

--- a/solution.py
+++ b/solution.py
@@ -92,7 +92,7 @@
         + jnp.einsum("ise,de->isd", grad_logits, router, preferred_element_type=jnp.float32)
     ).astype(jnp.bfloat16)
     router_term = jnp.einsum("isd,ise->de", tokens, grad_logits, preferred_element_type=jnp.float32)
-    grad_router = lax.psum(router_term, ("dp", "expert"))
+    grad_router = lax.psum(lax.psum(router_term, "expert"), "dp")
     return (mixed, grad_tokens, grad_router, grad_first, grad_second)
 
 

time: 498 us -> 617 us (1.24)
  waiting for transfers between devices: 349 us -> 469 us
    psum x1 -> x2, waiting for transfers between devices: 245 us -> 372 us  [local(): grad_router = lax.psum(lax.psum(router_term, 'expert'), 'dp')]
    all_gather x2, waiting for transfers between devices: 41.3 us -> 33.4 us  [to_owners(): return lax.all_gather(arrived, 'dp', axis=0, tiled=True)]
  transfers between devices with their start and end apart: 7 -> 8, of which waited for: 6 -> 7; matrix products, arithmetic and copies ran while one was open for 11% -> 11% of each run, Pallas kernels for 0% -> 0%
where the time goes in v1:
time: 617 us; the launch traced here: 616 us
  waiting for transfers between devices  469 us (76%)
  local copies, waits for them, and re-layouts  43.5 us (7%)
  matrix products  31.6 us (5%)
  blocking collectives  29.5 us (5%)
  starting transfers between devices  16.4 us (3%)
  between operations  14.3 us (2%)
  other arithmetic  11.6 us (2%)
    psum x2, waiting for transfers between devices, local(): grad_router = lax.psum(lax.psum(router_term, 'expert'), 'dp')  372 us
    reduce_scatter x2, waiting for transfers between devices, from_owners(): lax.psum_scatter(partial_value, 'dp', scatter_dimension=0, tiled=True)  58.2 us
    all_gather x2, waiting for transfers between devices, to_owners(): return lax.all_gather(arrived, 'dp', axis=0, tiled=True)  33.4 us
    all_to_all x2, blocking collectives, to_owners(): lax.all_to_all(local_rows, 'expert', split_axis=1, concat_axis=1, tiled=T...  29.5 us
    all_to_all x2, starting transfers between devices, from_owners(): lax.all_to_all(summed.astype(jnp.bfloat16), 'expert', split_axis=1, conca...  15.5 us
  transfers between devices with their start and end apart: 8, of which 7 were waited for; matrix products, arithmetic and copies ran while one was open for 11% of the time, Pallas kernels for 0%

profile of v1, /device:TPU:2, one launch (start us, length us, event | category | flops | bytes accessed | tf_op | source)
XLA Modules:
  0.0 616.0 jit_solution(365408758710342228)
XLA Ops:
  13.7 16.7 %all_to_all.20 = bf16[32,2,2048]{2,1,0:T(2,128)(2,1)S(1)} all-to-all(bf16[32,2,2048]{2,1,0:T(2,128)(2,1)S(1)} %reshape.119), channel_id=1, replica_groups=mesh['dp'=8,'expert'=32] {'expert'}, dimensions={0} | all-to-all | bytes 524288 | tf_op jit(solution)/shard_map/all_to_all | solution.py:27
  34.8 12.8 %all_to_all.21 = bf16[32,2,2048]{2,1,0:T(2,128)(2,1)S(1)} all-to-all(bf16[32,2,2048]{2,1,0:T(2,128)(2,1)S(1)} %reshape.123), channel_id=1, replica_groups=mesh['dp'=8,'expert'=32] {'expert'}, dimensions={0} | all-to-all | bytes 524288 | tf_op jit(solution)/shard_map/all_to_all | solution.py:27
  48.8 18.3 %all-gather.3.cloned.1.call-done = bf16[8,128,1024]{2,1,0:T(8,128)(2,1)} async-done(((bf16[1,128,1024]{2,1,0:T(8,128)(2,1)}), bf16[8,128,1024]{2,1,0:T(8,128)(2,1)}) %all-gather.3.cloned.1.call-update) | async-done | bytes 2097168 | tf_op jit(solution)/shard_map/all_gather | solution.py:28
  67.1 4.1 reshape.112
  71.2 4.3 copy.53
  75.5 5.5 fusion.13
  81.7 2.9 copy.44
  84.7 4.0 reshape.113
  88.9 15.1 %all-gather.5.cloned.1.call-done = bf16[8,128,1024]{2,1,0:T(8,128)(2,1)} async-done(((bf16[1,128,1024]{2,1,0:T(8,128)(2,1)}), bf16[8,128,1024]{2,1,0:T(8,128)(2,1)}) %all-gather.5.cloned.1.call-update) | async-done | bytes 2097168 | tf_op jit(solution)/shard_map/all_gather | solution.py:28
  104.0 4.1 reshape.116
  108.1 5.7 fusion.19
  114.6 2.9 copy.49
  117.6 4.0 reshape.117
  121.5 26.2 %reduce-scatter.3.cloned.1.call-done = bf16[1,128,1024]{2,1,0:T(8,128)(2,1)} async-done(((bf16[8,128,1024]{2,1,0:T(8,128)(2,1)}), bf16[1,128,1024]{2,1,0:T(8,128)(2,1)}) %reduce-scatter.3.cloned.1.call-update) | async-done | bytes 262160 | tf_op jit(solution)/shard_map/reduce_scatter | solution.py:31
  149.9 3.2 reduce.13
  153.9 7.3 %all-to-all-start.1 = ((bf16[32,2,2048]{2,1,0:T(2,128)(2,1)}), bf16[32,2,2048]{2,1,0:T(2,128)(2,1)S(1)}, u32[]{:S(2)}, u32[]{:S(2)}) async-start(bf16[32,2,2048]{2,1,0:T(2,128)(2,1)} %reshape.121), calls=%async_computation.2 | async-start | bytes 524288 | tf_op jit(solution)/shard_map/all_to_all | solution.py:34
  161.3 32.0 %reduce-scatter.5.cloned.1.call-done = bf16[1,128,1024]{2,1,0:T(8,128)(2,1)} async-done(((bf16[8,128,1024]{2,1,0:T(8,128)(2,1)}), bf16[1,128,1024]{2,1,0:T(8,128)(2,1)}) %reduce-scatter.5.cloned.1.call-update) | async-done | bytes 262160 | tf_op jit(solution)/shard_map/reduce_scatter | solution.py:31
  195.4 3.9 reduce.15
  201.1 8.2 %all-to-all-start.3 = ((bf16[32,2,2048]{2,1,0:T(2,128)(2,1)}), bf16[32,2,2048]{2,1,0:T(2,128)(2,1)}, u32[]{:S(2)}, u32[]{:S(2)}) async-start(bf16[32,2,2048]{2,1,0:T(2,128)(2,1)} %reshape.125), calls=%async_computation.5 | async-start | bytes 524288 | tf_op jit(solution)/shard_map/all_to_all | solution.py:34
  212.1 5.2 all-to-all-done.3
  217.3 2.8 reshape.126
  224.5 4.6 convolution_convert_fusion
  231.2 291.5 %all-reduce.3.cloned.1.call-done = f32[1024,128]{0,1:T(8,128)} async-done(((f32[1024,128]{0,1:T(8,128)}), f32[1024,128]{0,1:T(8,128)}) %all-reduce.3.cloned.1.call-update) | async-done | bytes 524304 | tf_op jit(solution)/shard_map/psum | solution.py:95
  526.5 80.6 %all-reduce.5.cloned.1.call-done = f32[1024,128]{0,1:T(8,128)} async-done(((f32[1024,128]{0,1:T(8,128)}), f32[1024,128]{0,1:T(8,128)}) %all-reduce.5.cloned.1.call-update) | async-done | bytes 524304 | tf_op jit(solution)/shard_map/psum | solution.py:95
  (63 shorter events, 35.8 us)
Async XLA Ops:
  7.2 68.3 %copy-start = (bf16[4,1024,256]{2,1,0:T(8,128)(2,1)S(1)}, bf16[4,1024,256]{2,1,0:T(8,128)(2,1)}, u32[]{:S(2)}) copy-start(bf16[4,1024,256]{2,1,0:T(8,128)(2,1)} %param.7) | copy-start | bytes 6291460
  7.2 59.9 %all-gather.3.cloned.1.call-start = ((), (), s32[]{:S(2)}) async-start(), calls=%async_computation.6 | async-start | bytes 2359296 | tf_op jit(solution)/shard_map/all_gather | solution.py:28
  10.4 21.2 %copy-start.2 = (bf16[1,256,1024]{2,1,0:T(8,128)(2,1)S(1)}, bf16[1,256,1024]{2,1,0:T(8,128)(2,1)}, u32[]{:S(2)}) copy-start(bf16[1,256,1024]{2,1,0:T(8,128)(2,1)} %param.9) | copy-start | bytes 1572868
  31.5 72.5 %all-gather.5.cloned.1.call-start = ((), (), s32[]{:S(2)}) async-start(), calls=%async_computation.8 | async-start | bytes 2359296 | tf_op jit(solution)/shard_map/all_gather | solution.py:28
  48.6 99.2 %reduce-scatter.3.cloned.1.call-start = ((), (), s32[]{:S(2)}) async-start(), calls=%async_computation.7 | async-start | bytes 2359296 | tf_op jit(solution)/shard_map/reduce_scatter | solution.py:31
  75.5 5.5 copy-start.4
  88.7 104.6 %reduce-scatter.5.cloned.1.call-start = ((), (), s32[]{:S(2)}) async-start(), calls=%async_computation.9 | async-start | bytes 2359296 | tf_op jit(solution)/shard_map/reduce_scatter | solution.py:31
  153.9 47.1 %all-to-all-start.1 = ((bf16[32,2,2048]{2,1,0:T(2,128)(2,1)}), bf16[32,2,2048]{2,1,0:T(2,128)(2,1)S(1)}, u32[]{:S(2)}, u32[]{:S(2)}) async-start(bf16[32,2,2048]{2,1,0:T(2,128)(2,1)} %reshape.121), calls=%async_computation.2 | async-start | bytes 524288 | tf_op jit(solution)/shard_map/all_to_all | solution.py:34
  201.1 16.2 %all-to-all-start.3 = ((bf16[32,2,2048]{2,1,0:T(2,128)(2,1)}), bf16[32,2,2048]{2,1,0:T(2,128)(2,1)}, u32[]{:S(2)}, u32[]{:S(2)}) async-start(bf16[32,2,2048]{2,1,0:T(2,128)(2,1)} %reshape.125), calls=%async_computation.5 | async-start | bytes 524288 | tf_op jit(solution)/shard_map/all_to_all | solution.py:34
  209.3 313.5 %all-reduce.3.cloned.1.call-start = ((), (), s32[]{:S(2)}) async-start(), calls=%async_computation.10 | async-start | bytes 1048576 | tf_op jit(solution)/shard_map/psum | solution.py:95
  221.6 0.6 copy-start.6
  221.6 0.6 copy-start.8
  224.5 382.7 %all-reduce.5.cloned.1.call-start = ((), (), s32[]{:S(2)}) async-start(), calls=%async_computation.11 | async-start | bytes 1048576 | tf_op jit(solution)/shard_map/psum | solution.py:95
  224.5 4.7 copy-start.1
  229.2 293.6 %copy-start.3 = (bf16[128,1,1024]{2,1,0:T(2,128)(2,1)S(1)}, bf16[128,1,1024]{2,1,0:T(2,128)(2,1)}, u32[]{:S(2)}) copy-start(bf16[128,1,1024]{2,1,0:T(2,128)(2,1)} %reshape.122) | copy-start | bytes 786436
  231.2 294.1 %copy-start.5 = (bf16[1024,128]{1,0:T(8,128)(2,1)S(1)}, bf16[1024,128]{1,0:T(8,128)(2,1)}, u32[]{:S(2)}) copy-start(bf16[1024,128]{1,0:T(8,128)(2,1)} %param.6) | copy-start | bytes 786436
  231.2 294.1 %copy-start.7 = (f32[256]{0:T(256)S(1)}, f32[256]{0:T(256)}, u32[]{:S(2)}) copy-start(f32[256]{0:T(256)} %copy-done.6) | copy-start | bytes 3076
  231.2 294.1 %copy-start.9 = (f32[128]{0:T(128)S(1)}, f32[128]{0:T(128)}, u32[]{:S(2)}) copy-start(f32[128]{0:T(128)} %copy-done.8) | copy-start | bytes 1540
Sparse Core Ops, SparseCore 0:
  31.7 35.4 all-gather.2
  69.6 34.4 all-gather.4
  106.6 41.1 reduce-scatter.2
  150.2 43.0 reduce-scatter.4
  224.6 298.1 all-reduce.2
  525.4 81.6 all-reduce.4
